TPU v7x, 128 devices: a whole 4x4x4 slice. The times are simulated.
128 devices in a mesh: dp: 32 (over y, z, core), section: 4 (over x).
Axes of the slice: x: 4, y: 4, z: 4, core: 2. Of those that a mesh axis runs over, the one named last changes fastest.
Arguments:
- hidden_in: bfloat16 [2, 2048, 8192], P(None, 'dp'), may hold values from -6 to 6
- out_grad: bfloat16 [2, 2048, 8192], P(None, 'dp'), may hold values from -0.4375 to 0.4375
- gains: float32 [2, 4, 4096], P(None, 'section'), may hold values from 0.1 to 1.9
- blocks: bfloat16 [2, 4, 256, 128, 128], P(None, 'section'), may hold values from -0.1875 to 0.1875
- block_rows: int32 [2, 4, 256], P(None, 'section'), may hold values from 0 to 31, as said below
- block_cols: int32 [2, 4, 256], P(None, 'section'), may hold values from 0 to 31, as said below
- block_counts: int32 [2, 4], P(None, 'section'), may hold values from 64 to 256, as said below
Outputs:
- block_grads: bfloat16 [2, 4, 256, 128, 128], P(None, 'section', 'dp')
Inputs may be any that keep to these rules, and one draw needn't show every extreme that they name: Slot n of layer (t, s) is the tile at block row block_rows[t, s, n]; the 256 slots of one layer name different tiles. `block_cols`: block column of each slot, paired with block_rows. `block_counts`: only slots below a layer's count hold weights; the others are padding. Counts differ between layers; in every draw one layer has 256 live slots and another a quarter of 256.
All inputs are finite; a program needn't handle non-finite values.
Results may differ from a plain program's by a relative error of at most 0.023.
Values may be sent and summed in bfloat16 or wider, within the bound.
No kernel may reach another device: no remote copies, remote signals or barrier semaphores. Data moves between devices by JAX's collectives and lax.ppermute only.
A program may use at most 320 MiB of HBM per device.

v0:
```python
import jax
import jax.numpy as jnp
from jax import lax
from jax.sharding import PartitionSpec as P

norm_eps = 1e-05
highest = lax.Precision.HIGHEST


def for_sending(shard):

    def short(part):
        return part.astype(jnp.bfloat16) if part.dtype == jnp.float32 else part

    return jax.tree.map(short, shard)


def from_behind(shard, axis, by):
    size = lax.axis_size(axis)
    return lax.ppermute(shard, axis, [(i, (i + by) % size) for i in range(size)])


def layer_tables(block_rows, block_cols, block_counts, turn_pos, grid_side):
    rows_list = block_rows[turn_pos, 0]
    cols_list = block_cols[turn_pos, 0]
    live_count = block_counts[turn_pos, 0]
    positions = jnp.arange(grid_side, dtype=jnp.int32)
    rows_match = (rows_list[:, None] == positions[None, :]).astype(jnp.float32)
    cols_match = (cols_list[:, None] == positions[None, :]).astype(jnp.float32)
    live_mask = (jnp.arange(rows_list.shape[0], dtype=jnp.int32) < live_count).astype(jnp.float32)
    return (
        rows_match.astype(jnp.bfloat16),
        cols_match.astype(jnp.bfloat16),
        rows_match * live_mask[:, None],
        cols_match * live_mask[:, None],
        live_mask,
        live_count,
    )


def tile_forward(normed3, weights, rows_hot, cols_live):
    gathered = jnp.einsum(
        "tgk,ng->tnk", normed3, rows_hot, preferred_element_type=jnp.float32
    ).astype(jnp.bfloat16)
    products = jnp.einsum("tnk,nkj->tnj", gathered, weights, preferred_element_type=jnp.float32)
    return jnp.einsum(
        "tnj,nc->tcj", products, cols_live, precision=highest, preferred_element_type=jnp.float32
    )


def tile_backward(normed3, error3, weights, rows_hot, cols_hot, rows_live, live_mask):
    gathered = jnp.einsum(
        "tgk,ng->tnk", normed3, rows_hot, preferred_element_type=jnp.float32
    ).astype(jnp.bfloat16)
    picked = jnp.einsum("tcj,nc->tnj", error3, cols_hot, preferred_element_type=jnp.float32).astype(
        jnp.bfloat16
    )
    products = jnp.einsum("tnj,nkj->tnk", picked, weights, preferred_element_type=jnp.float32)
    grad_normed = jnp.einsum(
        "tnk,ng->tgk", products, rows_live, precision=highest, preferred_element_type=jnp.float32
    )
    grad_tiles = jnp.einsum("tnk,tnj->nkj", gathered, picked, preferred_element_type=jnp.float32)
    return (grad_normed, grad_tiles * live_mask[:, None, None])


def sparse_forward(normed3, weights, tables):
    rows_hot, cols_hot, rows_live, cols_live, live_mask, live_count = tables
    return tile_forward(normed3, weights, rows_hot, cols_live)


def sparse_backward(normed3, error3, weights, tables, tile_total):
    rows_hot, cols_hot, rows_live, cols_live, live_mask, live_count = tables
    grad_normed, grad_tiles = tile_backward(
        normed3, error3, weights, rows_hot, cols_hot, rows_live, live_mask
    )
    return (grad_normed, tile_total + grad_tiles)


def body(hidden_in, out_grad, gains, blocks, block_rows, block_cols, block_counts):
    sections = lax.axis_size("section")
    section_pos = lax.axis_index("section")
    turn_count = blocks.shape[0]
    slot_count = blocks.shape[2]
    tile_side = blocks.shape[3]
    micro_count = hidden_in.shape[0]
    token_rows = hidden_in.shape[1]
    model_width = hidden_in.shape[2]
    half_width = model_width // 2
    grid_side = half_width // tile_side
    layer_total = turn_count * sections
    tick_count = micro_count + layer_total - 1
    tables = [
        layer_tables(block_rows, block_cols, block_counts, turn_pos, grid_side)
        for turn_pos in range(turn_count)
    ]

    def normalize(layer_in, turn_pos):
        parity = (turn_pos * sections + section_pos) % 2
        start_in = parity * half_width
        start_out = (1 - parity) * half_width
        as_float = layer_in.astype(jnp.float32)
        inv_rms = lax.rsqrt(jnp.mean(as_float * as_float, axis=-1, keepdims=True) + norm_eps)
        normed = (
            lax.dynamic_slice_in_dim(as_float, start_in, half_width, 1)
            * inv_rms
            * gains[turn_pos, 0]
        ).astype(jnp.bfloat16)
        return (as_float, inv_rms, normed, start_in, start_out)

    def forward_layer(layer_in, turn_pos):
        as_float, inv_rms, normed, start_in, start_out = normalize(layer_in, turn_pos)
        mixed_out = sparse_forward(
            normed.reshape(token_rows, grid_side, tile_side), blocks[turn_pos, 0], tables[turn_pos]
        )
        mixed_out = mixed_out.reshape(token_rows, half_width)
        updated = (
            lax.dynamic_slice_in_dim(as_float, start_out, half_width, 1) + jax.nn.silu(mixed_out)
        ).astype(jnp.bfloat16)
        return (lax.dynamic_update_slice_in_dim(layer_in, updated, start_out, 1), mixed_out)

    def forward_tick(carried, tick_pos):
        received, saved_inputs, saved_mixed = carried
        branch = jnp.int32(0)
        for turn_pos in range(turn_count):
            batch_pos = tick_pos - turn_pos * sections - section_pos
            active = (batch_pos >= 0) & (batch_pos < micro_count)
            branch = jnp.where(active, jnp.int32(turn_pos + 1), branch)

        def forward_resting(received, saved_inputs, saved_mixed):
            return (jnp.zeros_like(received), saved_inputs, saved_mixed)

        def forward_make_work(turn_pos):

            def forward_working(received, saved_inputs, saved_mixed):
                batch_pos = jnp.clip(
                    tick_pos - turn_pos * sections - section_pos, 0, micro_count - 1
                )
                if turn_pos == 0:
                    entering = lax.dynamic_index_in_dim(hidden_in, batch_pos, 0, keepdims=False)
                    layer_in = jnp.where(section_pos == 0, entering, received)
                else:
                    layer_in = received
                layer_out, mixed_out = forward_layer(layer_in, turn_pos)
                zero_pos = jnp.int32(0)
                saved_inputs = lax.dynamic_update_slice(
                    saved_inputs,
                    layer_in[None, None],
                    (jnp.int32(turn_pos), batch_pos, zero_pos, zero_pos),
                )
                saved_mixed = lax.dynamic_update_slice(
                    saved_mixed,
                    mixed_out[None, None],
                    (jnp.int32(turn_pos), batch_pos, zero_pos, zero_pos),
                )
                return (layer_out, saved_inputs, saved_mixed)

            return forward_working

        layer_out, saved_inputs, saved_mixed = lax.switch(
            branch,
            [forward_resting] + [forward_make_work(turn_pos) for turn_pos in range(turn_count)],
            received,
            saved_inputs,
            saved_mixed,
        )
        forwarded = jax.tree.map(
            lambda part, own: part.astype(own.dtype),
            from_behind(for_sending(layer_out), "section", 1),
            layer_out,
        )
        return ((forwarded, saved_inputs, saved_mixed), None)

    tick_list = jnp.arange(tick_count, dtype=jnp.int32)
    start_state = (
        jnp.zeros((token_rows, model_width), jnp.bfloat16),
        jnp.zeros((turn_count, micro_count, token_rows, model_width), jnp.bfloat16),
        jnp.zeros((turn_count, micro_count, token_rows, half_width), jnp.float32),
    )
    (received, saved_inputs, saved_mixed), unused_out = lax.scan(
        forward_tick, start_state, tick_list
    )

    def backward_layer(grad_in, turn_pos, batch_pos, tile_total):
        layer_in = lax.dynamic_index_in_dim(saved_inputs[turn_pos], batch_pos, 0, keepdims=False)
        mixed_out = lax.dynamic_index_in_dim(saved_mixed[turn_pos], batch_pos, 0, keepdims=False)
        as_float, inv_rms, normed, start_in, start_out = normalize(layer_in, turn_pos)
        upstream = grad_in.astype(jnp.float32)
        sigmoid_u = jax.nn.sigmoid(mixed_out)
        out_part = lax.dynamic_slice_in_dim(upstream, start_out, half_width, 1)
        tile_error = (out_part * sigmoid_u * (1.0 + mixed_out * (1.0 - sigmoid_u))).astype(
            jnp.bfloat16
        )
        grad_normed, tile_total = sparse_backward(
            normed.reshape(token_rows, grid_side, tile_side),
            tile_error.reshape(token_rows, grid_side, tile_side),
            blocks[turn_pos, 0],
            tables[turn_pos],
            tile_total,
        )
        weighted = grad_normed.reshape(token_rows, half_width) * gains[turn_pos, 0]
        in_part = lax.dynamic_slice_in_dim(as_float, start_in, half_width, 1)
        inner_sum = jnp.sum(weighted * in_part, axis=-1, keepdims=True)
        result = upstream - inv_rms * inv_rms * inv_rms / model_width * inner_sum * as_float
        in_result = lax.dynamic_slice_in_dim(result, start_in, half_width, 1) + inv_rms * weighted
        result = lax.dynamic_update_slice_in_dim(result, in_result, start_in, 1)
        return (result.astype(jnp.bfloat16), tile_total)

    def backward_tick(carried, tick_pos):
        received, grad_tiles = carried
        branch = jnp.int32(0)
        for turn_pos in range(turn_count):
            batch_pos = tick_pos - (layer_total - 1 - turn_pos * sections - section_pos)
            active = (batch_pos >= 0) & (batch_pos < micro_count)
            branch = jnp.where(active, jnp.int32(turn_pos + 1), branch)

        def backward_resting(received, grad_tiles):
            return (jnp.zeros_like(received), grad_tiles)

        def backward_make_work(turn_pos):

            def backward_working(received, grad_tiles):
                batch_pos = jnp.clip(
                    tick_pos - (layer_total - 1 - turn_pos * sections - section_pos),
                    0,
                    micro_count - 1,
                )
                if turn_pos == turn_count - 1:
                    entering = lax.dynamic_index_in_dim(out_grad, batch_pos, 0, keepdims=False)
                    grad_in = jnp.where(section_pos == sections - 1, entering, received)
                else:
                    grad_in = received
                result, tile_total = backward_layer(
                    grad_in, turn_pos, batch_pos, grad_tiles[turn_pos]
                )
                return (result, grad_tiles.at[turn_pos].set(tile_total))

            return backward_working

        result, grad_tiles = lax.switch(
            branch,
            [backward_resting] + [backward_make_work(turn_pos) for turn_pos in range(turn_count)],
            received,
            grad_tiles,
        )
        forwarded = jax.tree.map(
            lambda part, own: part.astype(own.dtype),
            from_behind(for_sending(result), "section", -1),
            result,
        )
        return ((forwarded, grad_tiles), None)

    start_back = (
        jnp.zeros((token_rows, model_width), jnp.bfloat16),
        jnp.zeros((turn_count, slot_count, tile_side, tile_side), jnp.float32),
    )
    (received, grad_tiles), unused_out = lax.scan(backward_tick, start_back, tick_list)
    summed = lax.psum_scatter(
        grad_tiles.astype(jnp.bfloat16), "dp", scatter_dimension=1, tiled=True
    )
    return summed[:, None]


def solution(mesh):
    return jax.shard_map(
        body,
        mesh=mesh,
        in_specs=(
            P(None, "dp", None),
            P(None, "dp", None),
            P(None, "section", None),
            P(None, "section", None, None, None),
            P(None, "section", None),
            P(None, "section", None),
            P(None, "section"),
        ),
        out_specs=P(None, "section", "dp", None, None),
        check_vma=False,
    )
```

profile of v0, /device:TPU:0, one launch (start us, length us, event | category | flops | bytes accessed | tf_op | source)
XLA Modules:
  0.0 1709.0 jit_solution(12762930211820573792)
XLA Ops:
  16.0 526.1 %while.37 = (s32[]{:T(128)}, bf16[64,8192]{1,0:T(8,128)(2,1)S(1)}, bf16[2,2,64,8192]{3,2,1,0:T(8,128)(2,1)}, f32[2,2,64,4096]{3,2,1,0:T(8,128)}, s32[9]{0:T(128)...) while((s32[]{:T(128)}, bf16[64,8192]{1,0:T(8,128)(2,1)S(1)}, ...), condition=%wide.region_6.7_spmd.clone, body=%wide.region_0.6_spmd.clone.sunk | while | flops 1483538560 | bytes 82581424 | solution.py:179
  18.1 36.1 %conditional.7 = (bf16[64,8192]{1,0:T(8,128)(2,1)}, bf16[2,2,64,8192]{3,2,1,0:T(8,128)(2,1)}, f32[2,2,64,4096]{3,2,1,0:T(8,128)}) conditional(s32[]{:T(128)} %clamp.15, (bf16[2,2,64,8192]{3,2,1,0:T(8,128)(2,1)}, f32[2,2,64,4096]{3,2,1,0:T(8,128)}) %tuple.112, (s32[]{:T(128)}, s32[]{:T(128)}, bf16[2,64,8192]{2,1,0:T(8,128)(2,1)}, ...), branch_computations={%region_1.1_spmd, %region_2.3_spmd, %region_4.5_spmd} | conditional | flops 1483489408 | bytes 78253432 | solution.py:159
  54.2 25.6 %collective-permute-done = bf16[64,8192]{1,0:T(8,128)(2,1)S(1)} collective-permute-done((bf16[64,8192]{1,0:T(8,128)(2,1)}, bf16[64,8192]{1,0:T(8,128)(2,1)S(1)}, u32[]{:S(2)}, u32[]{:S(2)}) %collective-permute-start) | collective-permute-done | bytes 1048608 | tf_op jit(solution)/shard_map/while/body/eval_jaxpr/ppermute | solution.py:20
  81.8 36.1 %conditional.7 = (bf16[64,8192]{1,0:T(8,128)(2,1)}, bf16[2,2,64,8192]{3,2,1,0:T(8,128)(2,1)}, f32[2,2,64,4096]{3,2,1,0:T(8,128)}) conditional(s32[]{:T(128)} %clamp.15, (bf16[2,2,64,8192]{3,2,1,0:T(8,128)(2,1)}, f32[2,2,64,4096]{3,2,1,0:T(8,128)}) %tuple.112, (s32[]{:T(128)}, s32[]{:T(128)}, bf16[2,64,8192]{2,1,0:T(8,128)(2,1)}, ...), branch_computations={%region_1.1_spmd, %region_2.3_spmd, %region_4.5_spmd} | conditional | flops 1483489408 | bytes 78253432 | solution.py:159
  145.8 34.1 %collective-permute-start = (bf16[64,8192]{1,0:T(8,128)(2,1)}, bf16[64,8192]{1,0:T(8,128)(2,1)S(1)}, u32[]{:S(2)}, u32[]{:S(2)}) collective-permute-start(bf16[64,8192]{1,0:T(8,128)(2,1)} %get-tuple-element.1005), channel_id=1, source_target_pairs={{0,1},{1,2},{2,3},{3,0},{4,5},{5,6},{6,7},{7,4},{8,9},{9,10},{10,1... | collective-permute-start | bytes 3145736 | tf_op jit(solution)/shard_map/while/body/eval_jaxpr/ppermute | solution.py:20
  205.9 54.2 %collective-permute-done = bf16[64,8192]{1,0:T(8,128)(2,1)S(1)} collective-permute-done((bf16[64,8192]{1,0:T(8,128)(2,1)}, bf16[64,8192]{1,0:T(8,128)(2,1)S(1)}, u32[]{:S(2)}, u32[]{:S(2)}) %collective-permute-start) | collective-permute-done | bytes 1048608 | tf_op jit(solution)/shard_map/while/body/eval_jaxpr/ppermute | solution.py:20
  262.1 34.1 %conditional.7 = (bf16[64,8192]{1,0:T(8,128)(2,1)}, bf16[2,2,64,8192]{3,2,1,0:T(8,128)(2,1)}, f32[2,2,64,4096]{3,2,1,0:T(8,128)}) conditional(s32[]{:T(128)} %clamp.15, (bf16[2,2,64,8192]{3,2,1,0:T(8,128)(2,1)}, f32[2,2,64,4096]{3,2,1,0:T(8,128)}) %tuple.112, (s32[]{:T(128)}, s32[]{:T(128)}, bf16[2,64,8192]{2,1,0:T(8,128)(2,1)}, ...), branch_computations={%region_1.1_spmd, %region_2.3_spmd, %region_4.5_spmd} | conditional | flops 1483489408 | bytes 78253432 | solution.py:159
  322.2 34.1 %conditional.7 = (bf16[64,8192]{1,0:T(8,128)(2,1)}, bf16[2,2,64,8192]{3,2,1,0:T(8,128)(2,1)}, f32[2,2,64,4096]{3,2,1,0:T(8,128)}) conditional(s32[]{:T(128)} %clamp.15, (bf16[2,2,64,8192]{3,2,1,0:T(8,128)(2,1)}, f32[2,2,64,4096]{3,2,1,0:T(8,128)}) %tuple.112, (s32[]{:T(128)}, s32[]{:T(128)}, bf16[2,64,8192]{2,1,0:T(8,128)(2,1)}, ...), branch_computations={%region_1.1_spmd, %region_2.3_spmd, %region_4.5_spmd} | conditional | flops 1483489408 | bytes 78253432 | solution.py:159
  381.6 32.0 %collective-permute-start = (bf16[64,8192]{1,0:T(8,128)(2,1)}, bf16[64,8192]{1,0:T(8,128)(2,1)S(1)}, u32[]{:S(2)}, u32[]{:S(2)}) collective-permute-start(bf16[64,8192]{1,0:T(8,128)(2,1)} %get-tuple-element.1005), channel_id=1, source_target_pairs={{0,1},{1,2},{2,3},{3,0},{4,5},{5,6},{6,7},{7,4},{8,9},{9,10},{10,1... | collective-permute-start | bytes 3145736 | tf_op jit(solution)/shard_map/while/body/eval_jaxpr/ppermute | solution.py:20
  437.0 48.7 %collective-permute-done = bf16[64,8192]{1,0:T(8,128)(2,1)S(1)} collective-permute-done((bf16[64,8192]{1,0:T(8,128)(2,1)}, bf16[64,8192]{1,0:T(8,128)(2,1)S(1)}, u32[]{:S(2)}, u32[]{:S(2)}) %collective-permute-start) | collective-permute-done | bytes 1048608 | tf_op jit(solution)/shard_map/while/body/eval_jaxpr/ppermute | solution.py:20
  491.2 50.9 %collective-permute-done = bf16[64,8192]{1,0:T(8,128)(2,1)S(1)} collective-permute-done((bf16[64,8192]{1,0:T(8,128)(2,1)}, bf16[64,8192]{1,0:T(8,128)(2,1)S(1)}, u32[]{:S(2)}, u32[]{:S(2)}) %collective-permute-start) | collective-permute-done | bytes 1048608 | tf_op jit(solution)/shard_map/while/body/eval_jaxpr/ppermute | solution.py:20
  553.4 992.1 %while.38 = (s32[]{:T(128)}, bf16[64,8192]{1,0:T(8,128)(2,1)S(1)}, f32[2,256,128,128]{3,2,1,0:T(8,128)}, s32[9]{0:T(128)S(1)}, s32[]{:T(128)}, /*index=5*/s32[]{...) while((s32[]{:T(128)}, bf16[64,8192]{1,0:T(8,128)(2,1)S(1)}, ...), condition=%wide.region_15.16_spmd.clone.clone, body=%wide.region_7.15_spmd.clone.clone.sunk | while | flops 2168047104 | bytes 231027536 | solution.py:256
  566.0 87.0 %collective-permute-start.1 = (bf16[64,8192]{1,0:T(8,128)(2,1)}, bf16[64,8192]{1,0:T(8,128)(2,1)S(1)}, u32[]{:S(2)}, u32[]{:S(2)}) collective-permute-start(bf16[64,8192]{1,0:T(8,128)(2,1)} %get-tuple-element.1034), channel_id=1, source_target_pairs={{0,3},{1,0},{2,1},{3,2},{4,7},{5,4},{6,5},{7,6},{8,11},{9,8},{10,9... | collective-permute-start | bytes 3145736 | tf_op jit(solution)/shard_map/while/body/eval_jaxpr/ppermute | solution.py:20
  673.0 94.5 %collective-permute-start.1 = (bf16[64,8192]{1,0:T(8,128)(2,1)}, bf16[64,8192]{1,0:T(8,128)(2,1)S(1)}, u32[]{:S(2)}, u32[]{:S(2)}) collective-permute-start(bf16[64,8192]{1,0:T(8,128)(2,1)} %get-tuple-element.1034), channel_id=1, source_target_pairs={{0,3},{1,0},{2,1},{3,2},{4,7},{5,4},{6,5},{7,6},{8,11},{9,8},{10,9... | collective-permute-start | bytes 3145736 | tf_op jit(solution)/shard_map/while/body/eval_jaxpr/ppermute | solution.py:20
  794.9 86.4 %collective-permute-done.1 = bf16[64,8192]{1,0:T(8,128)(2,1)S(1)} collective-permute-done((bf16[64,8192]{1,0:T(8,128)(2,1)}, bf16[64,8192]{1,0:T(8,128)(2,1)S(1)}, u32[]{:S(2)}, u32[]{:S(2)}) %collective-permute-start.1) | collective-permute-done | bytes 1048608 | tf_op jit(solution)/shard_map/while/body/eval_jaxpr/ppermute | solution.py:20
  884.6 86.6 %conditional.8 = (bf16[64,8192]{1,0:T(8,128)(2,1)}, f32[2,256,128,128]{3,2,1,0:T(8,128)}) conditional(s32[]{:T(128)} %clamp.16, f32[2,256,128,128]{3,2,1,0:T(8,128)} %get-tuple-element.1137, (bf16[64,8192]{1,0:T(8,128)(2,1)S(1)}, bf16[2,2,64,8192]{3,2,1,0:T(8,128)(2,1)}, s32[]{:T(128)}, s32[]{:T(128)}, ...), branch_computations={%region_8.8_spmd, %region_9.11_spmd, %region_12.14_spmd} | conditional | flops 2167947776 | bytes 226662608 | solution.py:239
  971.2 32.5 %collective-permute-done.1 = bf16[64,8192]{1,0:T(8,128)(2,1)S(1)} collective-permute-done((bf16[64,8192]{1,0:T(8,128)(2,1)}, bf16[64,8192]{1,0:T(8,128)(2,1)S(1)}, u32[]{:S(2)}, u32[]{:S(2)}) %collective-permute-start.1) | collective-permute-done | bytes 1048608 | tf_op jit(solution)/shard_map/while/body/eval_jaxpr/ppermute | solution.py:20
  1007.3 91.6 %conditional.8 = (bf16[64,8192]{1,0:T(8,128)(2,1)}, f32[2,256,128,128]{3,2,1,0:T(8,128)}) conditional(s32[]{:T(128)} %clamp.16, f32[2,256,128,128]{3,2,1,0:T(8,128)} %get-tuple-element.1137, (bf16[64,8192]{1,0:T(8,128)(2,1)S(1)}, bf16[2,2,64,8192]{3,2,1,0:T(8,128)(2,1)}, s32[]{:T(128)}, s32[]{:T(128)}, ...), branch_computations={%region_8.8_spmd, %region_9.11_spmd, %region_12.14_spmd} | conditional | flops 2167947776 | bytes 226662608 | solution.py:239
  1123.1 85.6 %collective-permute-start.1 = (bf16[64,8192]{1,0:T(8,128)(2,1)}, bf16[64,8192]{1,0:T(8,128)(2,1)S(1)}, u32[]{:S(2)}, u32[]{:S(2)}) collective-permute-start(bf16[64,8192]{1,0:T(8,128)(2,1)} %get-tuple-element.1034), channel_id=1, source_target_pairs={{0,3},{1,0},{2,1},{3,2},{4,7},{5,4},{6,5},{7,6},{8,11},{9,8},{10,9... | collective-permute-start | bytes 3145736 | tf_op jit(solution)/shard_map/while/body/eval_jaxpr/ppermute | solution.py:20
  1234.7 71.1 %collective-permute-done.1 = bf16[64,8192]{1,0:T(8,128)(2,1)S(1)} collective-permute-done((bf16[64,8192]{1,0:T(8,128)(2,1)}, bf16[64,8192]{1,0:T(8,128)(2,1)S(1)}, u32[]{:S(2)}, u32[]{:S(2)}) %collective-permute-start.1) | collective-permute-done | bytes 1048608 | tf_op jit(solution)/shard_map/while/body/eval_jaxpr/ppermute | solution.py:20
  1309.1 88.6 %conditional.8 = (bf16[64,8192]{1,0:T(8,128)(2,1)}, f32[2,256,128,128]{3,2,1,0:T(8,128)}) conditional(s32[]{:T(128)} %clamp.16, f32[2,256,128,128]{3,2,1,0:T(8,128)} %get-tuple-element.1137, (bf16[64,8192]{1,0:T(8,128)(2,1)S(1)}, bf16[2,2,64,8192]{3,2,1,0:T(8,128)(2,1)}, s32[]{:T(128)}, s32[]{:T(128)}, ...), branch_computations={%region_8.8_spmd, %region_9.11_spmd, %region_12.14_spmd} | conditional | flops 2167947776 | bytes 226662608 | solution.py:239
  1397.8 37.5 %collective-permute-done.1 = bf16[64,8192]{1,0:T(8,128)(2,1)S(1)} collective-permute-done((bf16[64,8192]{1,0:T(8,128)(2,1)}, bf16[64,8192]{1,0:T(8,128)(2,1)S(1)}, u32[]{:S(2)}, u32[]{:S(2)}) %collective-permute-start.1) | collective-permute-done | bytes 1048608 | tf_op jit(solution)/shard_map/while/body/eval_jaxpr/ppermute | solution.py:20
  1439.1 89.1 %conditional.8 = (bf16[64,8192]{1,0:T(8,128)(2,1)}, f32[2,256,128,128]{3,2,1,0:T(8,128)}) conditional(s32[]{:T(128)} %clamp.16, f32[2,256,128,128]{3,2,1,0:T(8,128)} %get-tuple-element.1137, (bf16[64,8192]{1,0:T(8,128)(2,1)S(1)}, bf16[2,2,64,8192]{3,2,1,0:T(8,128)(2,1)}, s32[]{:T(128)}, s32[]{:T(128)}, ...), branch_computations={%region_8.8_spmd, %region_9.11_spmd, %region_12.14_spmd} | conditional | flops 2167947776 | bytes 226662608 | solution.py:239
  1572.0 127.9 %reduce-scatter.5.cloned.1.call-done = bf16[8,32768]{1,0:T(8,128)(2,1)} async-done(((bf16[256,32768]{1,0:T(8,128)(2,1)}), bf16[8,32768]{1,0:T(8,128)(2,1)}) %reduce-scatter.5.cloned.1.call-update) | async-done | bytes 524304
  (357 shorter events, 766.1 us)
Async XLA Ops:
  6.5 1693.4 %reduce-scatter.5.cloned.1.call-start = ((), (), s32[]{:S(2)}) async-start(), calls=%async_computation.1 | async-start | bytes 17301504
  11.2 4.9 copy-start.9
  54.2 25.6 %collective-permute-start = (bf16[64,8192]{1,0:T(8,128)(2,1)}, bf16[64,8192]{1,0:T(8,128)(2,1)S(1)}, u32[]{:S(2)}, u32[]{:S(2)}) collective-permute-start(bf16[64,8192]{1,0:T(8,128)(2,1)} %get-tuple-element.1005), channel_id=1, source_target_pairs={{0,1},{1,2},{2,3},{3,0},{4,5},{5,6},{6,7},{7,4},{8,9},{9,10},{10,1... | collective-permute-start | bytes 3145736 | tf_op jit(solution)/shard_map/while/body/eval_jaxpr/ppermute | solution.py:20
  118.0 24.7 %collective-permute-start = (bf16[64,8192]{1,0:T(8,128)(2,1)}, bf16[64,8192]{1,0:T(8,128)(2,1)S(1)}, u32[]{:S(2)}, u32[]{:S(2)}) collective-permute-start(bf16[64,8192]{1,0:T(8,128)(2,1)} %get-tuple-element.1005), channel_id=1, source_target_pairs={{0,1},{1,2},{2,3},{3,0},{4,5},{5,6},{6,7},{7,4},{8,9},{9,10},{10,1... | collective-permute-start | bytes 3145736 | tf_op jit(solution)/shard_map/while/body/eval_jaxpr/ppermute | solution.py:20
  145.8 54.5 %collective-permute-start = (bf16[64,8192]{1,0:T(8,128)(2,1)}, bf16[64,8192]{1,0:T(8,128)(2,1)S(1)}, u32[]{:S(2)}, u32[]{:S(2)}) collective-permute-start(bf16[64,8192]{1,0:T(8,128)(2,1)} %get-tuple-element.1005), channel_id=1, source_target_pairs={{0,1},{1,2},{2,3},{3,0},{4,5},{5,6},{6,7},{7,4},{8,9},{9,10},{10,1... | collective-permute-start | bytes 3145736 | tf_op jit(solution)/shard_map/while/body/eval_jaxpr/ppermute | solution.py:20
  203.5 56.6 %collective-permute-start = (bf16[64,8192]{1,0:T(8,128)(2,1)}, bf16[64,8192]{1,0:T(8,128)(2,1)S(1)}, u32[]{:S(2)}, u32[]{:S(2)}) collective-permute-start(bf16[64,8192]{1,0:T(8,128)(2,1)} %get-tuple-element.1005), channel_id=1, source_target_pairs={{0,1},{1,2},{2,3},{3,0},{4,5},{5,6},{6,7},{7,4},{8,9},{9,10},{10,1... | collective-permute-start | bytes 3145736 | tf_op jit(solution)/shard_map/while/body/eval_jaxpr/ppermute | solution.py:20
  296.2 23.9 %collective-permute-start = (bf16[64,8192]{1,0:T(8,128)(2,1)}, bf16[64,8192]{1,0:T(8,128)(2,1)S(1)}, u32[]{:S(2)}, u32[]{:S(2)}) collective-permute-start(bf16[64,8192]{1,0:T(8,128)(2,1)} %get-tuple-element.1005), channel_id=1, source_target_pairs={{0,1},{1,2},{2,3},{3,0},{4,5},{5,6},{6,7},{7,4},{8,9},{9,10},{10,1... | collective-permute-start | bytes 3145736 | tf_op jit(solution)/shard_map/while/body/eval_jaxpr/ppermute | solution.py:20
  356.3 22.1 %collective-permute-start = (bf16[64,8192]{1,0:T(8,128)(2,1)}, bf16[64,8192]{1,0:T(8,128)(2,1)S(1)}, u32[]{:S(2)}, u32[]{:S(2)}) collective-permute-start(bf16[64,8192]{1,0:T(8,128)(2,1)} %get-tuple-element.1005), channel_id=1, source_target_pairs={{0,1},{1,2},{2,3},{3,0},{4,5},{5,6},{6,7},{7,4},{8,9},{9,10},{10,1... | collective-permute-start | bytes 3145736 | tf_op jit(solution)/shard_map/while/body/eval_jaxpr/ppermute | solution.py:20
  381.6 49.9 %collective-permute-start = (bf16[64,8192]{1,0:T(8,128)(2,1)}, bf16[64,8192]{1,0:T(8,128)(2,1)S(1)}, u32[]{:S(2)}, u32[]{:S(2)}) collective-permute-start(bf16[64,8192]{1,0:T(8,128)(2,1)} %get-tuple-element.1005), channel_id=1, source_target_pairs={{0,1},{1,2},{2,3},{3,0},{4,5},{5,6},{6,7},{7,4},{8,9},{9,10},{10,1... | collective-permute-start | bytes 3145736 | tf_op jit(solution)/shard_map/while/body/eval_jaxpr/ppermute | solution.py:20
  434.6 51.1 %collective-permute-start = (bf16[64,8192]{1,0:T(8,128)(2,1)}, bf16[64,8192]{1,0:T(8,128)(2,1)S(1)}, u32[]{:S(2)}, u32[]{:S(2)}) collective-permute-start(bf16[64,8192]{1,0:T(8,128)(2,1)} %get-tuple-element.1005), channel_id=1, source_target_pairs={{0,1},{1,2},{2,3},{3,0},{4,5},{5,6},{6,7},{7,4},{8,9},{9,10},{10,1... | collective-permute-start | bytes 3145736 | tf_op jit(solution)/shard_map/while/body/eval_jaxpr/ppermute | solution.py:20
  488.9 53.2 %collective-permute-start = (bf16[64,8192]{1,0:T(8,128)(2,1)}, bf16[64,8192]{1,0:T(8,128)(2,1)S(1)}, u32[]{:S(2)}, u32[]{:S(2)}) collective-permute-start(bf16[64,8192]{1,0:T(8,128)(2,1)} %get-tuple-element.1005), channel_id=1, source_target_pairs={{0,1},{1,2},{2,3},{3,0},{4,5},{5,6},{6,7},{7,4},{8,9},{9,10},{10,1... | collective-permute-start | bytes 3145736 | tf_op jit(solution)/shard_map/while/body/eval_jaxpr/ppermute | solution.py:20
  566.0 102.7 %collective-permute-start.1 = (bf16[64,8192]{1,0:T(8,128)(2,1)}, bf16[64,8192]{1,0:T(8,128)(2,1)S(1)}, u32[]{:S(2)}, u32[]{:S(2)}) collective-permute-start(bf16[64,8192]{1,0:T(8,128)(2,1)} %get-tuple-element.1034), channel_id=1, source_target_pairs={{0,3},{1,0},{2,1},{3,2},{4,7},{5,4},{6,5},{7,6},{8,11},{9,8},{10,9... | collective-permute-start | bytes 3145736 | tf_op jit(solution)/shard_map/while/body/eval_jaxpr/ppermute | solution.py:20
  673.0 109.2 %collective-permute-start.1 = (bf16[64,8192]{1,0:T(8,128)(2,1)}, bf16[64,8192]{1,0:T(8,128)(2,1)S(1)}, u32[]{:S(2)}, u32[]{:S(2)}) collective-permute-start(bf16[64,8192]{1,0:T(8,128)(2,1)} %get-tuple-element.1034), channel_id=1, source_target_pairs={{0,3},{1,0},{2,1},{3,2},{4,7},{5,4},{6,5},{7,6},{8,11},{9,8},{10,9... | collective-permute-start | bytes 3145736 | tf_op jit(solution)/shard_map/while/body/eval_jaxpr/ppermute | solution.py:20
  786.7 94.6 %collective-permute-start.1 = (bf16[64,8192]{1,0:T(8,128)(2,1)}, bf16[64,8192]{1,0:T(8,128)(2,1)S(1)}, u32[]{:S(2)}, u32[]{:S(2)}) collective-permute-start(bf16[64,8192]{1,0:T(8,128)(2,1)} %get-tuple-element.1034), channel_id=1, source_target_pairs={{0,3},{1,0},{2,1},{3,2},{4,7},{5,4},{6,5},{7,6},{8,11},{9,8},{10,9... | collective-permute-start | bytes 3145736 | tf_op jit(solution)/shard_map/while/body/eval_jaxpr/ppermute | solution.py:20
  916.0 10.6 copy-start.8
  971.1 32.6 %collective-permute-start.1 = (bf16[64,8192]{1,0:T(8,128)(2,1)}, bf16[64,8192]{1,0:T(8,128)(2,1)S(1)}, u32[]{:S(2)}, u32[]{:S(2)}) collective-permute-start(bf16[64,8192]{1,0:T(8,128)(2,1)} %get-tuple-element.1034), channel_id=1, source_target_pairs={{0,3},{1,0},{2,1},{3,2},{4,7},{5,4},{6,5},{7,6},{8,11},{9,8},{10,9... | collective-permute-start | bytes 3145736 | tf_op jit(solution)/shard_map/while/body/eval_jaxpr/ppermute | solution.py:20
  1043.7 10.6 copy-start.8
  1099.0 15.2 collective-permute-start.1
  1123.1 98.3 %collective-permute-start.1 = (bf16[64,8192]{1,0:T(8,128)(2,1)}, bf16[64,8192]{1,0:T(8,128)(2,1)S(1)}, u32[]{:S(2)}, u32[]{:S(2)}) collective-permute-start(bf16[64,8192]{1,0:T(8,128)(2,1)} %get-tuple-element.1034), channel_id=1, source_target_pairs={{0,3},{1,0},{2,1},{3,2},{4,7},{5,4},{6,5},{7,6},{8,11},{9,8},{10,9... | collective-permute-start | bytes 3145736 | tf_op jit(solution)/shard_map/while/body/eval_jaxpr/ppermute | solution.py:20
  1225.7 80.1 %collective-permute-start.1 = (bf16[64,8192]{1,0:T(8,128)(2,1)}, bf16[64,8192]{1,0:T(8,128)(2,1)S(1)}, u32[]{:S(2)}, u32[]{:S(2)}) collective-permute-start(bf16[64,8192]{1,0:T(8,128)(2,1)} %get-tuple-element.1034), channel_id=1, source_target_pairs={{0,3},{1,0},{2,1},{3,2},{4,7},{5,4},{6,5},{7,6},{8,11},{9,8},{10,9... | collective-permute-start | bytes 3145736 | tf_op jit(solution)/shard_map/while/body/eval_jaxpr/ppermute | solution.py:20
  1334.7 9.8 copy-start.7
  1397.7 37.5 %collective-permute-start.1 = (bf16[64,8192]{1,0:T(8,128)(2,1)}, bf16[64,8192]{1,0:T(8,128)(2,1)S(1)}, u32[]{:S(2)}, u32[]{:S(2)}) collective-permute-start(bf16[64,8192]{1,0:T(8,128)(2,1)} %get-tuple-element.1034), channel_id=1, source_target_pairs={{0,3},{1,0},{2,1},{3,2},{4,7},{5,4},{6,5},{7,6},{8,11},{9,8},{10,9... | collective-permute-start | bytes 3145736 | tf_op jit(solution)/shard_map/while/body/eval_jaxpr/ppermute | solution.py:20
  1464.8 9.8 copy-start.7
  1528.2 15.1 collective-permute-start.1
  (14 other events, 37.3 us)
Sparse Core Ops, SparseCore 0:
  1572.1 127.7 reduce-scatter.4
where the time goes:
time: 1710 us
  waiting for transfers between devices  717 us (42%)
  starting transfers between devices  358 us (21%)
  matrix products  261 us (15%)
  local copies, waits for them, and re-layouts  207 us (12%)
  loops' own time  81.6 us (5%)
  other arithmetic  70.9 us (4%)
    ppermute x18, waiting for transfers between devices, from_behind(): lax.ppermute(shard, axis, [(i, (i + by) % size) for i in range(size)])  589 us
    ppermute x18, starting transfers between devices, from_behind(): lax.ppermute(shard, axis, [(i, (i + by) % size) for i in range(size)])  358 us
    unnamed x2, waiting for transfers between devices  128 us
    dot_general x4, matrix products, tile_backward(): jnp.einsum('tnk,tnj->nkj', gathered, picked, preferred_element_type=jnp.f...  71.3 us
    another operation x9, loops' own time, backward_tick(): lax.switch(branch, [backward_resting] + [backward_make_work(turn_pos) for...  48.7 us
    slice x4, local copies, waits for them, and re-layouts, backward_working(): grad_tiles[turn_pos]  46.5 us
    dot_general x4, matrix products, tile_backward(): jnp.einsum('tnj,nkj->tnk', picked, weights, preferred_element_type=jnp.fl...  42 us
    dot_general x4, matrix products, tile_backward(): jnp.einsum('tnk,ng->tgk', products, rows_live, precision=highest, preferr...  40.7 us
  transfers between devices with their start and end apart: 19, of which 19 were waited for; matrix products, arithmetic and copies ran while one was open for 0% of the time, Pallas kernels for 0%

commit v1 on v0

v1 whole, which is shorter than its diff:
```python
import jax
import jax.numpy as jnp
from jax import lax
from jax.experimental import pallas as pl
from jax.experimental.pallas import tpu as pltpu
from jax.sharding import PartitionSpec as P

norm_eps = 1e-05
LAG = 1
UNROLL = 32
f32 = jnp.float32
bf16 = jnp.bfloat16
VM = pl.BlockSpec(memory_space=pltpu.VMEM)
SM = pl.BlockSpec(memory_space=pltpu.SMEM)
ANY = pl.BlockSpec(memory_space=pl.ANY)
LIMIT = 48 * 2**20


def split_pair(value, width):
    high = value.astype(bf16).astype(f32)
    low = value - high
    lane = lax.broadcasted_iota(jnp.int32, (value.shape[0], width), 1)
    return jnp.where(lane == 0, high, jnp.where(lane == 1, low, 0.0)).astype(bf16)


def tile_loop(table, turn, slots, groups, gather_at, scatter_at, source, weights, acc, transposed):
    dims = (((1,), (1 if transposed else 0,)), ((), ()))

    def group(g, carry):
        for k in range(UNROLL):
            n = turn * slots + g * UNROLL + k
            got = table[gather_at + n]
            put = table[scatter_at + n]
            acc[put] += lax.dot_general(source[got], weights[n], dims, preferred_element_type=f32)
        return carry

    lax.fori_loop(0, groups, group, 0)


class Plan:
    def __init__(self, sections, turns, slots, tile, grid, tokens):
        self.sections, self.turns, self.slots = sections, turns, slots
        self.tile, self.grid = tile, grid
        self.units = sections * LAG
        self.rows = tokens // self.units
        self.span = (sections - 1) * LAG
        self.ticks = turns * self.units + self.span
        self.row_get, self.col_get = 0, turns * slots
        self.row_put, self.col_put = 2 * turns * slots, 3 * turns * slots
        self.groups = 4 * turns * slots
        self.counts = self.groups + turns
        self.section = self.counts + turns
        self.half = self.section + 1

    def piece(self, dtype, extra=0):
        return jax.ShapeDtypeStruct((self.grid + extra, self.rows, self.tile), dtype)


def forward_tick(plan, tick, table, entering, square0, gains, weights, prev, critical, early, stores):
    G, T, B, M = plan.grid, plan.rows, plan.tile, plan.units
    width = 2 * G * B
    use_entering = tick < M + plan.span
    use_prev = tick >= M
    named = dict(table=table, entering=entering if use_entering else None, square0=square0 if tick < M else None,
                 gains=gains, weights=weights, prev=prev if use_prev else None, critical=critical, early=early)
    names = [name for name in named if named[name] is not None]
    turns_here = [turn for turn in range(2) if (use_entering if turn == 0 else use_prev)]
    count_in = len(names)

    def kernel(*refs):
        ref = dict(zip(names, refs))
        store_out = dict(zip(turns_here, refs[count_in + len(turns_here) + 4:]))
        sent, kept, slope, scale = refs[count_in + len(turns_here):][:4]
        normed, acc, sem = refs[-3:]
        tab = ref["table"]
        step = tick - LAG * tab[plan.section]
        active = (step >= 0) & (step < 2 * M)

        @pl.when(active)
        def _():
            turn = jnp.where(step >= M, 1, 0)
            unit = step - turn * M
            squares = jnp.zeros((T, B), f32)
            for b in range(G):
                cut = slice(b * B, (b + 1) * B)
                if use_entering:
                    value = ref["entering"][unit, :, cut].astype(f32)
                if use_prev:
                    older = ref["prev"][b].astype(f32)
                    value = jnp.where(turn == 0, value, older) if use_entering else older
                if early is not None:
                    value = value + ref["early"][b].astype(f32)
                if critical is not None:
                    value = value + ref["critical"][b].astype(f32)
                value = value.astype(bf16)
                kept[b] = value
                value = value.astype(f32)
                squares = squares + value * value
            own = jnp.sum(squares, axis=-1, keepdims=True)
            total = own
            if critical is not None:
                total = total + jnp.sum(ref["critical"][G].astype(f32), axis=-1, keepdims=True)
            if tick < M:
                total = total + jnp.sum(ref["square0"][unit], axis=-1, keepdims=True)
            inv_rms = lax.rsqrt(total / width + norm_eps)
            scale[...] = jnp.broadcast_to(inv_rms, (T, B))
            for b in range(G):
                gain = ref["gains"][turn * G + b]
                normed[b] = (kept[b].astype(f32) * inv_rms * gain).astype(bf16)
            for place in turns_here:
                @pl.when(turn == place)
                def _():
                    pltpu.make_async_copy(normed, store_out[place].at[unit], sem).start()
            acc[...] = jnp.zeros_like(acc)
            tile_loop(tab, turn, plan.slots, tab[plan.groups + turn], plan.row_get, plan.col_put, normed, ref["weights"], acc, False)
            pltpu.make_async_copy(normed, store_out[turns_here[0]].at[unit], sem).wait()
            for b in range(G):
                mixed = acc[b]
                gate = jax.nn.sigmoid(mixed)
                sent[b] = (mixed * gate).astype(bf16)
                slope[b] = (gate * (1.0 + mixed * (1.0 - gate))).astype(bf16)
            sent[G] = split_pair(own, B)

        @pl.when(jnp.logical_not(active))
        def _():
            sent[...] = jnp.zeros_like(sent)

    ins = [named[name] for name in names] + [stores[turn] for turn in turns_here]
    outs = pl.pallas_call(
        kernel,
        in_specs=[SM] + [VM] * (count_in - 1) + [ANY] * len(turns_here),
        out_specs=[VM] * 4 + [ANY] * len(turns_here),
        out_shape=[plan.piece(bf16, 1), plan.piece(bf16), plan.piece(bf16), jax.ShapeDtypeStruct((T, B), f32)]
        + [jax.ShapeDtypeStruct(stores[turn].shape, bf16) for turn in turns_here],
        input_output_aliases={count_in + i: 4 + i for i in range(len(turns_here))},
        scratch_shapes=[pltpu.VMEM((G, T, B), bf16), pltpu.VMEM((G + 1, T, B), f32), pltpu.SemaphoreType.DMA],
        compiler_params=pltpu.CompilerParams(vmem_limit_bytes=LIMIT),
        name="forward_tick",
    )(*ins)
    stores = list(stores)
    for i, turn in enumerate(turns_here):
        stores[turn] = outs[4 + i]
    return outs[0], (outs[1], outs[2], outs[3]), stores


def backward_tick(plan, tick, table, entering, gains, weights, saved, prev, critical, early, stores):
    G, T, B, M = plan.grid, plan.rows, plan.tile, plan.units
    width = 2 * G * B
    back = plan.ticks - 1 - tick
    use_entering = back < M + plan.span
    use_prev = back >= M
    named = dict(table=table, entering=entering if use_entering else None, gains=gains, weights=weights,
                 kept=saved[0], slope=saved[1], scale=saved[2],
                 prev=prev if use_prev else None, critical=critical, early=early)
    names = [name for name in named if named[name] is not None]
    turns_here = [turn for turn in range(2) if (use_entering if turn == 1 else use_prev)]
    count_in = len(names)

    def kernel(*refs):
        ref = dict(zip(names, refs))
        sent, grad = refs[count_in + len(turns_here):][:2]
        store_out = dict(zip(turns_here, refs[count_in + len(turns_here) + 2:]))
        error, acc, sem = refs[-3:]
        tab = ref["table"]
        step = tick - LAG * tab[plan.section]
        active = (step >= 0) & (step < 2 * M)

        @pl.when(active)
        def _():
            turn = jnp.where(step >= M, 1, 0)
            unit = step - turn * M
            for b in range(G):
                cut = slice(b * B, (b + 1) * B)
                if use_entering:
                    value = ref["entering"][unit, :, cut].astype(f32)
                if use_prev:
                    older = ref["prev"][b].astype(f32)
                    value = jnp.where(turn == 1, value, older) if use_entering else older
                if early is not None:
                    value = value + ref["early"][b].astype(f32)
                if critical is not None:
                    value = value + ref["critical"][b].astype(f32)
                value = value.astype(bf16)
                grad[b] = value
                error[b] = (value.astype(f32) * ref["slope"][b].astype(f32)).astype(bf16)
            for place in turns_here:
                @pl.when(turn == place)
                def _():
                    pltpu.make_async_copy(error, store_out[place].at[unit], sem).start()
            acc[...] = jnp.zeros_like(acc)
            tile_loop(tab, turn, plan.slots, tab[plan.groups + turn], plan.col_get, plan.row_put, error, ref["weights"], acc, True)
            pltpu.make_async_copy(error, store_out[turns_here[0]].at[unit], sem).wait()
            inner = jnp.zeros((T, B), f32)
            for b in range(G):
                weighted = acc[b] * ref["gains"][turn * G + b]
                acc[b] = weighted
                inner = inner + weighted * ref["kept"][b].astype(f32)
            inv_rms = ref["scale"][:, 0:1]
            own = inv_rms * inv_rms * inv_rms / width * jnp.sum(inner, axis=-1, keepdims=True)
            total = own
            if critical is not None:
                total = total + jnp.sum(ref["critical"][G].astype(f32), axis=-1, keepdims=True)
            for b in range(G):
                sent[b] = (inv_rms * acc[b] - total * ref["kept"][b].astype(f32)).astype(bf16)
            sent[G] = split_pair(own, B)

        @pl.when(jnp.logical_not(active))
        def _():
            sent[...] = jnp.zeros_like(sent)

    ins = [named[name] for name in names] + [stores[turn] for turn in turns_here]
    outs = pl.pallas_call(
        kernel,
        in_specs=[SM] + [VM] * (count_in - 1) + [ANY] * len(turns_here),
        out_specs=[VM] * 2 + [ANY] * len(turns_here),
        out_shape=[plan.piece(bf16, 1), plan.piece(bf16)]
        + [jax.ShapeDtypeStruct(stores[turn].shape, bf16) for turn in turns_here],
        input_output_aliases={count_in + i: 2 + i for i in range(len(turns_here))},
        scratch_shapes=[pltpu.VMEM((G, T, B), bf16), pltpu.VMEM((G + 1, T, B), f32), pltpu.SemaphoreType.DMA],
        compiler_params=pltpu.CompilerParams(vmem_limit_bytes=LIMIT),
        name="backward_tick",
    )(*ins)
    stores = list(stores)
    for i, turn in enumerate(turns_here):
        stores[turn] = outs[2 + i]
    return outs[0], outs[1], stores


def tile_grads(plan, turn, table, normed_pair, error_pair, share, parts):
    G, T, B, M = plan.grid, plan.rows, plan.tile, plan.units
    local = plan.slots // parts
    steps = 8
    chunk = local // steps
    tokens = M * T

    def kernel(tab, *refs):
        normeds, errors = refs[:parts], refs[parts:2 * parts]
        out, turned, flat = refs[2 * parts:]
        step = pl.program_id(0)

        @pl.when(step == 0)
        def _():
            for b in range(G):
                for p in range(parts):
                    for m in range(M):
                        at = p * tokens + m * T
                        flat[b, at:at + T, :] = errors[p][m, b]
                    whole = jnp.concatenate([normeds[p][m, b] for m in range(M)], axis=0)
                    turned[b, :, p * tokens:(p + 1) * tokens] = whole.T

        half = tab[plan.half]
        live = tab[plan.counts + turn]
        for k in range(chunk):
            i = step * chunk + k
            n = (i // share) * (share * parts) + half * share + i % share
            at = turn * plan.slots + n
            made = jnp.dot(turned[tab[plan.row_get + at]], flat[tab[plan.col_get + at]], preferred_element_type=f32)
            out[k] = jnp.where(n < live, made, 0.0).astype(bf16)

    whole = pl.BlockSpec((M, G, T, B), lambda i, tab: (0, 0, 0, 0))
    return pl.pallas_call(
        kernel,
        grid_spec=pltpu.PrefetchScalarGridSpec(
            num_scalar_prefetch=1,
            grid=(steps,),
            in_specs=[whole] * (2 * parts),
            out_specs=pl.BlockSpec((chunk, B, B), lambda i, tab: (i, 0, 0)),
            scratch_shapes=[pltpu.VMEM((G, B, parts * tokens), bf16), pltpu.VMEM((G, parts * tokens, B), bf16)],
        ),
        out_shape=jax.ShapeDtypeStruct((local, B, B), bf16),
        compiler_params=pltpu.CompilerParams(vmem_limit_bytes=LIMIT),
        name="tile_grads",
    )(table, *normed_pair, *error_pair)


def body(hidden_in, out_grad, gains, blocks, block_rows, block_cols, block_counts):
    sections = lax.axis_size("section")
    replicas = lax.axis_size("dp")
    section_pos = lax.axis_index("section").astype(jnp.int32)
    core = (lax.axis_index("dp") % 2).astype(jnp.int32)
    turns, slots, tile = blocks.shape[0], blocks.shape[2], blocks.shape[3]
    tokens = hidden_in.shape[0] * hidden_in.shape[1]
    half_width = hidden_in.shape[2] // 2
    grid = half_width // tile
    plan = Plan(sections, turns, slots, tile, grid, tokens)
    M, T = plan.units, plan.rows

    rows_list, cols_list, counts = block_rows[:, 0], block_cols[:, 0], block_counts[:, 0]
    live = jnp.arange(slots, dtype=jnp.int32)[None] < counts[:, None]
    table = jnp.concatenate([
        rows_list.reshape(-1), cols_list.reshape(-1),
        jnp.where(live, rows_list, grid).reshape(-1), jnp.where(live, cols_list, grid).reshape(-1),
        (counts + UNROLL - 1) // UNROLL, counts, section_pos[None], core[None],
    ])
    parity = section_pos % 2
    hidden = hidden_in.reshape(M, T, 2 * half_width)
    entering = lax.dynamic_slice_in_dim(hidden, parity * half_width, half_width, 2)
    entering_grad = lax.dynamic_slice_in_dim(
        out_grad.reshape(M, T, 2 * half_width), (1 - parity) * half_width, half_width, 2
    )
    other = hidden[:, :, half_width:].astype(f32)
    square0 = jnp.where(section_pos == 0, jnp.sum(other * other, axis=-1, keepdims=True), 0.0)
    square0 = jnp.pad(square0, ((0, 0), (0, 0), (0, tile - 1)))
    weights = blocks.reshape(turns * slots, tile, tile)
    gain_rows = gains.reshape(turns * grid, 1, tile)

    def ring(part, by):
        return lax.ppermute(part, "section", [(i, (i + by) % sections) for i in range(sections)])

    empty = jnp.zeros((M, grid, T, tile), bf16)
    stores = [empty, empty]
    ahead, behind, saved = {}, {}, {}
    for tick in range(plan.ticks):
        prev = saved[tick - M][0] if tick >= M else None
        sent, saved[tick], stores = forward_tick(
            plan, tick, table, entering, square0, gain_rows, weights, prev,
            ahead.get(tick - LAG), behind.get(tick - plan.span), stores,
        )
        if tick + LAG < plan.ticks:
            ahead[tick] = ring(sent, 1)
        if tick + plan.span < plan.ticks:
            behind[tick] = ring(sent, -1)
    normed = stores

    swap = [(i, i ^ 1) for i in range(replicas)]
    share = slots // replicas

    def finish(turn, error):
        pairs = []
        for own in (normed[turn], error):
            other_core = lax.ppermute(own, "dp", swap)
            pairs.append([own, other_core])
        part = tile_grads(plan, turn, table, pairs[0], pairs[1], share, 2)
        groups = [[i for i in range(replicas) if i % 2 == c] for c in range(2)]
        return lax.psum_scatter(part, "dp", scatter_dimension=0, axis_index_groups=groups, tiled=True)

    stores = [empty, empty]
    ahead, behind, grads = {}, {}, {}
    results = [None] * turns
    for back in range(plan.ticks):
        tick = plan.ticks - 1 - back
        sent, grads[back], stores = backward_tick(
            plan, tick, table, entering_grad, gain_rows, weights, saved[tick], grads.get(back - M),
            ahead.get(back - LAG), behind.get(back - plan.span), stores,
        )
        if back + LAG < plan.ticks:
            ahead[back] = ring(sent, -1)
        if back + plan.span < plan.ticks:
            behind[back] = ring(sent, 1)
        if back == M + plan.span - 1:
            results[1] = finish(1, stores[1])
    results[0] = finish(0, stores[0])
    return jnp.stack(results)[:, None]


def solution(mesh):
    return jax.shard_map(
        body,
        mesh=mesh,
        in_specs=(
            P(None, "dp", None),
            P(None, "dp", None),
            P(None, "section", None),
            P(None, "section", None, None, None),
            P(None, "section", None),
            P(None, "section", None),
            P(None, "section"),
        ),
        out_specs=P(None, "section", "dp", None, None),
        check_vma=False,
    )
```

time: 1710 us -> 524 us (0.31)
  waiting for transfers between devices: 717 us -> 187 us
  matrix products: 261 us -> 0 us
  starting transfers between devices: 358 us -> 98 us
  Pallas kernels: 0 us -> 208 us
  local copies, waits for them, and re-layouts: 207 us -> 18.7 us
  loops' own time: 81.6 us -> 0 us
  other arithmetic: 70.9 us -> 4.95 us
    ppermute x18 -> x40, waiting for transfers between devices: 589 us -> 108 us  [the longest x36 103 us: ring(): lax.ppermute(part, 'section', [(i, (i + by) % sections) for i in range(se...]
    dot_general x32 -> x0, matrix products: 261 us -> none  [the longest x4 71.3 us: tile_backward(): jnp.einsum('tnk,tnj->nkj', gathered, picked, preferred_element_type=jnp.f...]
    ppermute x18 -> x40, starting transfers between devices: 358 us -> 98 us  [the longest x36 97.8 us: ring(): lax.ppermute(part, 'section', [(i, (i + by) % sections) for i in range(se...]
    pallas_call x0 -> x24, Pallas kernels: none -> 208 us  [the longest x11 109 us: backward_tick(): pl.pallas_call(kernel, in_specs=[SM] + [VM] * (count_in - 1) + [ANY] * le...]
    unnamed x2, waiting for transfers between devices: 128 us -> 0.03 us
    another operation x20 -> x0, loops' own time: 81.6 us -> none  [the longest x9 48.7 us: backward_tick(): lax.switch(branch, [backward_resting] + [backward_make_work(turn_pos) for...]
    reduce_scatter x0 -> x2, waiting for transfers between devices: none -> 78.8 us  [finish(): lax.psum_scatter(part, 'dp', scatter_dimension=0, axis_index_groups=group...]
    slice x23 -> x0, local copies, waits for them, and re-layouts: 54.1 us -> none  [the longest x4 46.5 us: backward_working(): grad_tiles[turn_pos]]
  transfers between devices with their start and end apart: 19 -> 42, of which waited for: 19 -> 23; matrix products, arithmetic and copies ran while one was open for 0% -> 0% of each run, Pallas kernels for 0% -> 31%
where the time goes in v1:
time: 524 us; the launch traced here: 531 us
  Pallas kernels  208 us (40%)
  waiting for transfers between devices  187 us (36%)
  starting transfers between devices  98 us (19%)
  local copies, waits for them, and re-layouts  18.7 us (4%)
  between operations  14.4 us (3%)
    pallas_call x11, Pallas kernels, backward_tick(): pl.pallas_call(kernel, in_specs=[SM] + [VM] * (count_in - 1) + [ANY] * le...  109 us
    ppermute x36, waiting for transfers between devices, ring(): lax.ppermute(part, 'section', [(i, (i + by) % sections) for i in range(se...  103 us
    ppermute x36, starting transfers between devices, ring(): lax.ppermute(part, 'section', [(i, (i + by) % sections) for i in range(se...  97.8 us
    pallas_call x11, Pallas kernels, forward_tick(): pl.pallas_call(kernel, in_specs=[SM] + [VM] * (count_in - 1) + [ANY] * le...  85.7 us
    reduce_scatter x2, waiting for transfers between devices, finish(): lax.psum_scatter(part, 'dp', scatter_dimension=0, axis_index_groups=group...  78.8 us
    unnamed x130, local copies, waits for them, and re-layouts  16.5 us
    pallas_call x2, Pallas kernels, tile_grads(): pl.pallas_call(kernel, grid_spec=pltpu.PrefetchScalarGridSpec(num_scalar_...  13.7 us
  transfers between devices with their start and end apart: 42, of which 23 were waited for; matrix products, arithmetic and copies ran while one was open for 0% of the time, Pallas kernels for 31%

profile of v1, /device:TPU:0, one launch (start us, length us, event | category | flops | bytes accessed | tf_op | source)
XLA Modules:
  0.0 530.7 jit_solution(3293394319026218777)
XLA Ops:
  11.5 9.4 %forward_tick.11 = (bf16[33,32,128]{2,1,0:T(8,128)(2,1)S(1)}, bf16[32,32,128]{2,1,0:T(8,128)(2,1)S(1)}, bf16[32,32,128]{2,1,0:T(8,128)(2,1)S(1)}, f32[32,128]{1,0:T(8,128)S(1)}, bf16[4,32,32,128]{3,2,1,0:T(8,128)(2,1)S(1)}) custom-call(s32[2054]{0:T(1024)S(1)} %concatenate.3.refs_0_.tab, ...), custom_call_target="tpu_custom_call", output_to_operand_aliasing={{4}: (5, {})} | custom-call | tf_op jit(solution)/shard_map/forward_tick/pallas_call | solution.py:129
  21.6 8.7 %collective-permute-done.refs_5_ = bf16[33,32,128]{2,1,0:T(8,128)(2,1)S(1)} collective-permute-done((bf16[33,32,128]{2,1,0:T(8,128)(2,1)S(1)}, bf16[33,32,128]{2,1,0:T(8,128)(2,1)S(1)}, u32[]{:S(2)}, u32[]{:S(2)}) %collective-permute-start) | collective-permute-done | bytes 270368 | tf_op jit(solution)/shard_map/ppermute | solution.py:308
  30.3 9.4 %forward_tick.12 = (bf16[33,32,128]{2,1,0:T(8,128)(2,1)S(1)}, bf16[32,32,128]{2,1,0:T(8,128)(2,1)S(1)}, bf16[32,32,128]{2,1,0:T(8,128)(2,1)S(1)}, f32[32,128]{1,0:T(8,128)S(1)}, bf16[4,32,32,128]{3,2,1,0:T(8,128)(2,1)S(1)}) custom-call(s32[2054]{0:T(1024)S(1)} %concatenate.3.refs_0_.tab, ...), custom_call_target="tpu_custom_call", output_to_operand_aliasing={{4}: (6, {})} | custom-call | tf_op jit(solution)/shard_map/forward_tick/pallas_call | solution.py:129
  47.6 9.4 %forward_tick.13 = (bf16[33,32,128]{2,1,0:T(8,128)(2,1)S(1)}, bf16[32,32,128]{2,1,0:T(8,128)(2,1)S(1)}, bf16[32,32,128]{2,1,0:T(8,128)(2,1)S(1)}, f32[32,128]{1,0:T(8,128)S(1)}, bf16[4,32,32,128]{3,2,1,0:T(8,128)(2,1)S(1)}) custom-call(s32[2054]{0:T(1024)S(1)} %concatenate.3.refs_0_.tab, ...), custom_call_target="tpu_custom_call", output_to_operand_aliasing={{4}: (6, {})} | custom-call | tf_op jit(solution)/shard_map/forward_tick/pallas_call | solution.py:129
  65.4 9.4 %forward_tick.14 = (bf16[33,32,128]{2,1,0:T(8,128)(2,1)S(1)}, bf16[32,32,128]{2,1,0:T(8,128)(2,1)S(1)}, bf16[32,32,128]{2,1,0:T(8,128)(2,1)S(1)}, f32[32,128]{1,0:T(8,128)S(1)}, bf16[4,32,32,128]{3,2,1,0:T(8,128)(2,1)S(1)}) custom-call(s32[2054]{0:T(1024)S(1)} %concatenate.3.refs_0_.tab, ...), custom_call_target="tpu_custom_call", output_to_operand_aliasing={{4}: (7, {})} | custom-call | tf_op jit(solution)/shard_map/forward_tick/pallas_call | solution.py:129
  116.2 7.8 %forward_tick.17 = (bf16[33,32,128]{2,1,0:T(8,128)(2,1)}, bf16[32,32,128]{2,1,0:T(8,128)(2,1)S(1)}, bf16[32,32,128]{2,1,0:T(8,128)(2,1)S(1)}, f32[32,128]{1,0:T(...) custom-call(s32[2054]{0:T(1024)S(1)} %concatenate.3.refs_0_.tab, ...), custom_call_target="tpu_custom_call", output_to_operand_aliasing={{4}: (7, {}), {5}: (8, {})} | custom-call | tf_op jit(solution)/shard_map/forward_tick/pallas_call | solution.py:129
  176.9 9.5 %collective-permute-done.17.refs_4_ = bf16[33,32,128]{2,1,0:T(8,128)(2,1)S(1)} collective-permute-done((bf16[33,32,128]{2,1,0:T(8,128)(2,1)S(1)}, bf16[33,32,128]{2,1,0:T(8,128)(2,1)S(1)}, u32[]{:S(2)}, u32[]{:S(2)}) %collective-permute-start.17) | collective-permute-done | bytes 270368 | tf_op jit(solution)/shard_map/ppermute | solution.py:308
  198.9 11.4 %collective-permute-start.19 = (bf16[33,32,128]{2,1,0:T(8,128)(2,1)S(1)}, bf16[33,32,128]{2,1,0:T(8,128)(2,1)S(1)}, u32[]{:S(2)}, u32[]{:S(2)}) collective-permute-start(bf16[33,32,128]{2,1,0:T(8,128)(2,1)S(1)} %get-tuple-element.136), channel_id=1, source_target_pairs={{0,3},{1,0},{2,1},{3,2},{4,7},{5,4},{6,5},{7,6},{8,11},{9,8},{10,9... | collective-permute-start | bytes 811016 | tf_op jit(solution)/shard_map/ppermute | solution.py:308
  220.2 9.5 %collective-permute-start.20 = (bf16[33,32,128]{2,1,0:T(8,128)(2,1)S(1)}, bf16[33,32,128]{2,1,0:T(8,128)(2,1)S(1)}, u32[]{:S(2)}, u32[]{:S(2)}) collective-permute-start(bf16[33,32,128]{2,1,0:T(8,128)(2,1)S(1)} %get-tuple-element.138), channel_id=1, source_target_pairs={{0,3},{1,0},{2,1},{3,2},{4,7},{5,4},{6,5},{7,6},{8,11},{9,8},{10,9... | collective-permute-start | bytes 811016 | tf_op jit(solution)/shard_map/ppermute | solution.py:308
  239.7 9.5 %collective-permute-start.21 = (bf16[33,32,128]{2,1,0:T(8,128)(2,1)S(1)}, bf16[33,32,128]{2,1,0:T(8,128)(2,1)S(1)}, u32[]{:S(2)}, u32[]{:S(2)}) collective-permute-start(bf16[33,32,128]{2,1,0:T(8,128)(2,1)S(1)} %get-tuple-element.150), channel_id=1, source_target_pairs={{0,3},{1,0},{2,1},{3,2},{4,7},{5,4},{6,5},{7,6},{8,11},{9,8},{10,9... | collective-permute-start | bytes 811016 | tf_op jit(solution)/shard_map/ppermute | solution.py:308
  253.2 7.7 %backward_tick.14 = (bf16[33,32,128]{2,1,0:T(8,128)(2,1)S(1)}, bf16[32,32,128]{2,1,0:T(8,128)(2,1)S(1)}, bf16[4,32,32,128]{3,2,1,0:T(8,128)(2,1)S(1)}) custom-call(s32[2054]{0:T(1024)S(1)} %concatenate.3.refs_0_.tab, bf16[4,32,4096]{2,1,0:T(8,128)(2,1)S(1)} %constant_dynamic-slice_fusion.refs_1_, ...), custom_call_target="tpu_custom_call", output_to_operand_aliasing={{2}: (9, {})} | custom-call | tf_op jit(solution)/shard_map/backward_tick/pallas_call | solution.py:212
  261.6 7.7 %collective-permute-start.23 = (bf16[33,32,128]{2,1,0:T(8,128)(2,1)S(1)}, bf16[33,32,128]{2,1,0:T(8,128)(2,1)S(1)}, u32[]{:S(2)}, u32[]{:S(2)}) collective-permute-start(bf16[33,32,128]{2,1,0:T(8,128)(2,1)S(1)} %get-tuple-element.152), channel_id=1, source_target_pairs={{0,3},{1,0},{2,1},{3,2},{4,7},{5,4},{6,5},{7,6},{8,11},{9,8},{10,9... | collective-permute-start | bytes 811016 | tf_op jit(solution)/shard_map/ppermute | solution.py:308
  273.4 17.4 %backward_tick.15 = (bf16[33,32,128]{2,1,0:T(8,128)(2,1)S(1)}, bf16[32,32,128]{2,1,0:T(8,128)(2,1)S(1)}, bf16[4,32,32,128]{3,2,1,0:T(8,128)(2,1)S(1)}, bf16[4,32,32,128]{3,2,1,0:T(8,128)(2,1)S(1)}) custom-call(s32[2054]{0:T(1024)S(1)} %concatenate.3.refs_0_.tab, ...), custom_call_target="tpu_custom_call", output_to_operand_aliasing={{2}: (10, {}), {3}: (11, {})} | custom-call | tf_op jit(solution)/shard_map/backward_tick/pallas_call | solution.py:212
  290.9 7.8 %collective-permute-start.25 = (bf16[33,32,128]{2,1,0:T(8,128)(2,1)S(1)}, bf16[33,32,128]{2,1,0:T(8,128)(2,1)S(1)}, u32[]{:S(2)}, u32[]{:S(2)}) collective-permute-start(bf16[33,32,128]{2,1,0:T(8,128)(2,1)S(1)} %get-tuple-element.154), channel_id=1, source_target_pairs={{0,3},{1,0},{2,1},{3,2},{4,7},{5,4},{6,5},{7,6},{8,11},{9,8},{10,9... | collective-permute-start | bytes 811016 | tf_op jit(solution)/shard_map/ppermute | solution.py:308
  303.6 7.8 %backward_tick.16 = (bf16[33,32,128]{2,1,0:T(8,128)(2,1)S(1)}, bf16[32,32,128]{2,1,0:T(8,128)(2,1)S(1)}, bf16[4,32,32,128]{3,2,1,0:T(8,128)(2,1)S(1)}, bf16[4,32,32,128]{3,2,1,0:T(8,128)(2,1)S(1)}) custom-call(s32[2054]{0:T(1024)S(1)} %concatenate.3.refs_0_.tab, ...), custom_call_target="tpu_custom_call", output_to_operand_aliasing={{2}: (10, {}), {3}: (11, {})} | custom-call | tf_op jit(solution)/shard_map/backward_tick/pallas_call | solution.py:212
  312.1 7.7 %collective-permute-start.27 = (bf16[33,32,128]{2,1,0:T(8,128)(2,1)S(1)}, bf16[33,32,128]{2,1,0:T(8,128)(2,1)S(1)}, u32[]{:S(2)}, u32[]{:S(2)}) collective-permute-start(bf16[33,32,128]{2,1,0:T(8,128)(2,1)S(1)} %get-tuple-element.157), channel_id=1, source_target_pairs={{0,3},{1,0},{2,1},{3,2},{4,7},{5,4},{6,5},{7,6},{8,11},{9,8},{10,9... | collective-permute-start | bytes 811016 | tf_op jit(solution)/shard_map/ppermute | solution.py:308
  323.8 7.7 %backward_tick.17 = (bf16[33,32,128]{2,1,0:T(8,128)(2,1)S(1)}, bf16[32,32,128]{2,1,0:T(8,128)(2,1)S(1)}, bf16[4,32,32,128]{3,2,1,0:T(8,128)(2,1)S(1)}, bf16[4,32,32,128]{3,2,1,0:T(8,128)(2,1)S(1)}) custom-call(s32[2054]{0:T(1024)S(1)} %concatenate.3.refs_0_.tab, ...), custom_call_target="tpu_custom_call", output_to_operand_aliasing={{2}: (10, {}), {3}: (11, {})} | custom-call | tf_op jit(solution)/shard_map/backward_tick/pallas_call | solution.py:212
  343.5 7.8 %collective-permute-start.29 = (bf16[33,32,128]{2,1,0:T(8,128)(2,1)}, bf16[33,32,128]{2,1,0:T(8,128)(2,1)S(1)}, u32[]{:S(2)}, u32[]{:S(2)}) collective-permute-start(bf16[33,32,128]{2,1,0:T(8,128)(2,1)} %copy-done.59), channel_id=1, source_target_pairs={{0,3},{1,0},{2,1},{3,2},{4,7},{5,4},{6,5},{7,6},{8,11},{9,8},{10,9... | collective-permute-start | bytes 811016 | tf_op jit(solution)/shard_map/ppermute | solution.py:308
  351.3 7.4 %collective-permute-done.30.refs_8_ = bf16[33,32,128]{2,1,0:T(8,128)(2,1)S(1)} collective-permute-done((bf16[33,32,128]{2,1,0:T(8,128)(2,1)}, bf16[33,32,128]{2,1,0:T(8,128)(2,1)S(1)}, u32[]{:S(2)}, u32[]{:S(2)}) %collective-permute-start.30) | collective-permute-done | bytes 270368 | tf_op jit(solution)/shard_map/ppermute | solution.py:308
  361.6 12.5 %backward_tick.18 = (bf16[33,32,128]{2,1,0:T(8,128)(2,1)S(1)}, bf16[32,32,128]{2,1,0:T(8,128)(2,1)}, bf16[4,32,32,128]{3,2,1,0:T(8,128)(2,1)S(1)}) custom-call(s32[2054]{0:T(1024)S(1)} %concatenate.3.refs_0_.tab, f32[64,1,128]{2,1,0:T(1,128)S(1)} %bitcast.37, bf16[512,128,128]{2,1,0:T(8,128)(2,1)} %bitcast.59, ...), custom_call_target="tpu_custom_call", output_to_operand_aliasing={{2}: (9, {})} | custom-call | tf_op jit(solution)/shard_map/backward_tick/pallas_call | solution.py:212
  382.0 12.7 %backward_tick.19 = (bf16[33,32,128]{2,1,0:T(8,128)(2,1)S(1)}, bf16[32,32,128]{2,1,0:T(8,128)(2,1)}, bf16[4,32,32,128]{3,2,1,0:T(8,128)(2,1)S(1)}) custom-call(s32[2054]{0:T(1024)S(1)} %concatenate.3.refs_0_.tab, f32[64,1,128]{2,1,0:T(1,128)S(1)} %bitcast.38, bf16[512,128,128]{2,1,0:T(8,128)(2,1)} %bitcast.60, ...), custom_call_target="tpu_custom_call", output_to_operand_aliasing={{2}: (9, {})} | custom-call | tf_op jit(solution)/shard_map/backward_tick/pallas_call | solution.py:212
  401.7 12.6 %backward_tick.20 = (bf16[33,32,128]{2,1,0:T(8,128)(2,1)S(1)}, bf16[32,32,128]{2,1,0:T(8,128)(2,1)}, bf16[4,32,32,128]{3,2,1,0:T(8,128)(2,1)S(1)}) custom-call(s32[2054]{0:T(1024)S(1)} %concatenate.3.refs_0_.tab, f32[64,1,128]{2,1,0:T(1,128)S(1)} %bitcast.39, bf16[512,128,128]{2,1,0:T(8,128)(2,1)} %bitcast.61, ...), custom_call_target="tpu_custom_call", output_to_operand_aliasing={{2}: (9, {})} | custom-call | tf_op jit(solution)/shard_map/backward_tick/pallas_call | solution.py:212
  420.8 12.5 %backward_tick.21 = (bf16[33,32,128]{2,1,0:T(8,128)(2,1)}, bf16[32,32,128]{2,1,0:T(8,128)(2,1)}, bf16[4,32,32,128]{3,2,1,0:T(8,128)(2,1)S(1)}) custom-call(s32[2054]{0:T(1024)S(1)} %concatenate.3.refs_0_.tab, f32[64,1,128]{2,1,0:T(1,128)S(1)} %bitcast.40, bf16[512,128,128]{2,1,0:T(8,128)(2,1)} %bitcast.62, ...), custom_call_target="tpu_custom_call", output_to_operand_aliasing={{2}: (9, {})} | custom-call | tf_op jit(solution)/shard_map/backward_tick/pallas_call | solution.py:212
  443.0 78.8 %reduce-scatter.3.cloned.1.call-done = bf16[8,128,128]{2,1,0:T(8,128)(2,1)} async-done(((bf16[128,128,128]{2,1,0:T(8,128)(2,1)}), bf16[8,128,128]{2,1,0:T(8,128)(2,1)}) %reduce-scatter.3.cloned.1.call-update) | async-done | bytes 262160 | tf_op jit(solution)/shard_map/reduce_scatter | solution.py:335
  (232 shorter events, 214.2 us)
Async XLA Ops:
  6.5 436.5 %reduce-scatter.5.cloned.1.call-start = ((), (), s32[]{:S(2)}) async-start(), calls=%async_computation.3 | async-start | bytes 4456448 | tf_op jit(solution)/shard_map/reduce_scatter | solution.py:335
  39.8 21.1 %collective-permute-start.3 = (bf16[33,32,128]{2,1,0:T(8,128)(2,1)S(1)}, bf16[33,32,128]{2,1,0:T(8,128)(2,1)S(1)}, u32[]{:S(2)}, u32[]{:S(2)}) collective-permute-start(bf16[33,32,128]{2,1,0:T(8,128)(2,1)S(1)} %get-tuple-element.93), channel_id=1, source_target_pairs={{0,3},{1,0},{2,1},{3,2},{4,7},{5,4},{6,5},{7,6},{8,11},{9,8},{10,9... | collective-permute-start | bytes 811016 | tf_op jit(solution)/shard_map/ppermute | solution.py:308
  57.7 21.0 %collective-permute-start.5 = (bf16[33,32,128]{2,1,0:T(8,128)(2,1)S(1)}, bf16[33,32,128]{2,1,0:T(8,128)(2,1)S(1)}, u32[]{:S(2)}, u32[]{:S(2)}) collective-permute-start(bf16[33,32,128]{2,1,0:T(8,128)(2,1)S(1)} %get-tuple-element.95), channel_id=1, source_target_pairs={{0,3},{1,0},{2,1},{3,2},{4,7},{5,4},{6,5},{7,6},{8,11},{9,8},{10,9... | collective-permute-start | bytes 811016 | tf_op jit(solution)/shard_map/ppermute | solution.py:308
  75.5 20.1 %collective-permute-start.7 = (bf16[33,32,128]{2,1,0:T(8,128)(2,1)S(1)}, bf16[33,32,128]{2,1,0:T(8,128)(2,1)S(1)}, u32[]{:S(2)}, u32[]{:S(2)}) collective-permute-start(bf16[33,32,128]{2,1,0:T(8,128)(2,1)S(1)} %get-tuple-element.100), channel_id=1, source_target_pairs={{0,3},{1,0},{2,1},{3,2},{4,7},{5,4},{6,5},{7,6},{8,11},{9,8},{10,9... | collective-permute-start | bytes 811016 | tf_op jit(solution)/shard_map/ppermute | solution.py:308
  92.3 19.4 %collective-permute-start.9 = (bf16[33,32,128]{2,1,0:T(8,128)(2,1)S(1)}, bf16[33,32,128]{2,1,0:T(8,128)(2,1)S(1)}, u32[]{:S(2)}, u32[]{:S(2)}) collective-permute-start(bf16[33,32,128]{2,1,0:T(8,128)(2,1)S(1)} %get-tuple-element.102), channel_id=1, source_target_pairs={{0,3},{1,0},{2,1},{3,2},{4,7},{5,4},{6,5},{7,6},{8,11},{9,8},{10,9... | collective-permute-start | bytes 811016 | tf_op jit(solution)/shard_map/ppermute | solution.py:308
  109.7 19.0 %collective-permute-start.12 = (bf16[33,32,128]{2,1,0:T(8,128)(2,1)S(1)}, bf16[33,32,128]{2,1,0:T(8,128)(2,1)S(1)}, u32[]{:S(2)}, u32[]{:S(2)}) collective-permute-start(bf16[33,32,128]{2,1,0:T(8,128)(2,1)S(1)} %get-tuple-element.104), channel_id=1, source_target_pairs={{0,3},{1,0},{2,1},{3,2},{4,7},{5,4},{6,5},{7,6},{8,11},{9,8},{10,9... | collective-permute-start | bytes 811016 | tf_op jit(solution)/shard_map/ppermute | solution.py:308
  126.5 19.5 %collective-permute-start.14 = (bf16[33,32,128]{2,1,0:T(8,128)(2,1)S(1)}, bf16[33,32,128]{2,1,0:T(8,128)(2,1)S(1)}, u32[]{:S(2)}, u32[]{:S(2)}) collective-permute-start(bf16[33,32,128]{2,1,0:T(8,128)(2,1)S(1)} %get-tuple-element.107), channel_id=1, source_target_pairs={{0,3},{1,0},{2,1},{3,2},{4,7},{5,4},{6,5},{7,6},{8,11},{9,8},{10,9... | collective-permute-start | bytes 811016 | tf_op jit(solution)/shard_map/ppermute | solution.py:308
  144.0 20.5 %collective-permute-start.16 = (bf16[33,32,128]{2,1,0:T(8,128)(2,1)}, bf16[33,32,128]{2,1,0:T(8,128)(2,1)}, u32[]{:S(2)}, u32[]{:S(2)}) collective-permute-start(bf16[33,32,128]{2,1,0:T(8,128)(2,1)} %get-tuple-element.117), channel_id=1, source_target_pairs={{0,3},{1,0},{2,1},{3,2},{4,7},{5,4},{6,5},{7,6},{8,11},{9,8},{10,9... | collective-permute-start | bytes 811016 | tf_op jit(solution)/shard_map/ppermute | solution.py:308
  162.7 14.2 %collective-permute-start.18 = (bf16[33,32,128]{2,1,0:T(8,128)(2,1)}, bf16[33,32,128]{2,1,0:T(8,128)(2,1)S(1)}, u32[]{:S(2)}, u32[]{:S(2)}) collective-permute-start(bf16[33,32,128]{2,1,0:T(8,128)(2,1)} %copy-done.61), channel_id=1, source_target_pairs={{0,3},{1,0},{2,1},{3,2},{4,7},{5,4},{6,5},{7,6},{8,11},{9,8},{10,9... | collective-permute-start | bytes 811016 | tf_op jit(solution)/shard_map/ppermute | solution.py:308
  198.9 15.4 %collective-permute-start.19 = (bf16[33,32,128]{2,1,0:T(8,128)(2,1)S(1)}, bf16[33,32,128]{2,1,0:T(8,128)(2,1)S(1)}, u32[]{:S(2)}, u32[]{:S(2)}) collective-permute-start(bf16[33,32,128]{2,1,0:T(8,128)(2,1)S(1)} %get-tuple-element.136), channel_id=1, source_target_pairs={{0,3},{1,0},{2,1},{3,2},{4,7},{5,4},{6,5},{7,6},{8,11},{9,8},{10,9... | collective-permute-start | bytes 811016 | tf_op jit(solution)/shard_map/ppermute | solution.py:308
  220.2 13.5 %collective-permute-start.20 = (bf16[33,32,128]{2,1,0:T(8,128)(2,1)S(1)}, bf16[33,32,128]{2,1,0:T(8,128)(2,1)S(1)}, u32[]{:S(2)}, u32[]{:S(2)}) collective-permute-start(bf16[33,32,128]{2,1,0:T(8,128)(2,1)S(1)} %get-tuple-element.138), channel_id=1, source_target_pairs={{0,3},{1,0},{2,1},{3,2},{4,7},{5,4},{6,5},{7,6},{8,11},{9,8},{10,9... | collective-permute-start | bytes 811016 | tf_op jit(solution)/shard_map/ppermute | solution.py:308
  229.8 19.5 %collective-permute-start.22 = (bf16[33,32,128]{2,1,0:T(8,128)(2,1)S(1)}, bf16[33,32,128]{2,1,0:T(8,128)(2,1)S(1)}, u32[]{:S(2)}, u32[]{:S(2)}) collective-permute-start(bf16[33,32,128]{2,1,0:T(8,128)(2,1)S(1)} %get-tuple-element.136), channel_id=1, source_target_pairs={{0,1},{1,2},{2,3},{3,0},{4,5},{5,6},{6,7},{7,4},{8,9},{9,10},{10,1... | collective-permute-start | bytes 811016 | tf_op jit(solution)/shard_map/ppermute | solution.py:308
  239.7 13.5 %collective-permute-start.21 = (bf16[33,32,128]{2,1,0:T(8,128)(2,1)S(1)}, bf16[33,32,128]{2,1,0:T(8,128)(2,1)S(1)}, u32[]{:S(2)}, u32[]{:S(2)}) collective-permute-start(bf16[33,32,128]{2,1,0:T(8,128)(2,1)S(1)} %get-tuple-element.150), channel_id=1, source_target_pairs={{0,3},{1,0},{2,1},{3,2},{4,7},{5,4},{6,5},{7,6},{8,11},{9,8},{10,9... | collective-permute-start | bytes 811016 | tf_op jit(solution)/shard_map/ppermute | solution.py:308
  249.2 20.1 %collective-permute-start.24 = (bf16[33,32,128]{2,1,0:T(8,128)(2,1)S(1)}, bf16[33,32,128]{2,1,0:T(8,128)(2,1)S(1)}, u32[]{:S(2)}, u32[]{:S(2)}) collective-permute-start(bf16[33,32,128]{2,1,0:T(8,128)(2,1)S(1)} %get-tuple-element.138), channel_id=1, source_target_pairs={{0,1},{1,2},{2,3},{3,0},{4,5},{5,6},{6,7},{7,4},{8,9},{9,10},{10,1... | collective-permute-start | bytes 811016 | tf_op jit(solution)/shard_map/ppermute | solution.py:308
  269.3 29.4 %collective-permute-start.26 = (bf16[33,32,128]{2,1,0:T(8,128)(2,1)S(1)}, bf16[33,32,128]{2,1,0:T(8,128)(2,1)S(1)}, u32[]{:S(2)}, u32[]{:S(2)}) collective-permute-start(bf16[33,32,128]{2,1,0:T(8,128)(2,1)S(1)} %get-tuple-element.150), channel_id=1, source_target_pairs={{0,1},{1,2},{2,3},{3,0},{4,5},{5,6},{6,7},{7,4},{8,9},{9,10},{10,1... | collective-permute-start | bytes 811016 | tf_op jit(solution)/shard_map/ppermute | solution.py:308
  298.6 21.2 %collective-permute-start.28 = (bf16[33,32,128]{2,1,0:T(8,128)(2,1)S(1)}, bf16[33,32,128]{2,1,0:T(8,128)(2,1)S(1)}, u32[]{:S(2)}, u32[]{:S(2)}) collective-permute-start(bf16[33,32,128]{2,1,0:T(8,128)(2,1)S(1)} %get-tuple-element.152), channel_id=1, source_target_pairs={{0,1},{1,2},{2,3},{3,0},{4,5},{5,6},{6,7},{7,4},{8,9},{9,10},{10,1... | collective-permute-start | bytes 811016 | tf_op jit(solution)/shard_map/ppermute | solution.py:308
  319.8 14.1 %collective-permute-start.38 = (bf16[4,32,32,128]{3,2,1,0:T(8,128)(2,1)S(1)}, bf16[4,32,32,128]{3,2,1,0:T(8,128)(2,1)S(1)}, u32[]{:S(2)}, u32[]{:S(2)}) collective-permute-start(bf16[4,32,32,128]{3,2,1,0:T(8,128)(2,1)S(1)} %get-tuple-element.179.refs_0_), channel_id=1, source_target_pairs={{0,4},{4,0},{8,12},{12,8},{16,20},{20,16},{24,28},{28,24},{32,36},... | collective-permute-start | bytes 3145736 | tf_op jit(solution)/shard_map/ppermute | solution.py:331
  343.4 178.4 %reduce-scatter.3.cloned.1.call-start = ((), (), s32[]{:S(2)}) async-start(), calls=%async_computation.2 | async-start | bytes 4456448 | tf_op jit(solution)/shard_map/reduce_scatter | solution.py:335
  343.5 15.2 %collective-permute-start.30 = (bf16[33,32,128]{2,1,0:T(8,128)(2,1)}, bf16[33,32,128]{2,1,0:T(8,128)(2,1)S(1)}, u32[]{:S(2)}, u32[]{:S(2)}) collective-permute-start(bf16[33,32,128]{2,1,0:T(8,128)(2,1)} %copy-done.57), channel_id=1, source_target_pairs={{0,1},{1,2},{2,3},{3,0},{4,5},{5,6},{6,7},{7,4},{8,9},{9,10},{10,1... | collective-permute-start | bytes 811016 | tf_op jit(solution)/shard_map/ppermute | solution.py:308
  343.5 15.2 %collective-permute-start.29 = (bf16[33,32,128]{2,1,0:T(8,128)(2,1)}, bf16[33,32,128]{2,1,0:T(8,128)(2,1)S(1)}, u32[]{:S(2)}, u32[]{:S(2)}) collective-permute-start(bf16[33,32,128]{2,1,0:T(8,128)(2,1)} %copy-done.59), channel_id=1, source_target_pairs={{0,3},{1,0},{2,1},{3,2},{4,7},{5,4},{6,5},{7,6},{8,11},{9,8},{10,9... | collective-permute-start | bytes 811016 | tf_op jit(solution)/shard_map/ppermute | solution.py:308
  351.3 25.5 %collective-permute-start.32 = (bf16[33,32,128]{2,1,0:T(8,128)(2,1)}, bf16[33,32,128]{2,1,0:T(8,128)(2,1)S(1)}, u32[]{:S(2)}, u32[]{:S(2)}) collective-permute-start(bf16[33,32,128]{2,1,0:T(8,128)(2,1)} %copy-done.58), channel_id=1, source_target_pairs={{0,1},{1,2},{2,3},{3,0},{4,5},{5,6},{6,7},{7,4},{8,9},{9,10},{10,1... | collective-permute-start | bytes 811016 | tf_op jit(solution)/shard_map/ppermute | solution.py:308
  376.8 20.1 %collective-permute-start.34 = (bf16[33,32,128]{2,1,0:T(8,128)(2,1)S(1)}, bf16[33,32,128]{2,1,0:T(8,128)(2,1)S(1)}, u32[]{:S(2)}, u32[]{:S(2)}) collective-permute-start(bf16[33,32,128]{2,1,0:T(8,128)(2,1)S(1)} %copy-done.60), channel_id=1, source_target_pairs={{0,1},{1,2},{2,3},{3,0},{4,5},{5,6},{6,7},{7,4},{8,9},{9,10},{10,1... | collective-permute-start | bytes 811016 | tf_op jit(solution)/shard_map/ppermute | solution.py:308
  394.9 19.6 %collective-permute-start.36 = (bf16[33,32,128]{2,1,0:T(8,128)(2,1)S(1)}, bf16[33,32,128]{2,1,0:T(8,128)(2,1)S(1)}, u32[]{:S(2)}, u32[]{:S(2)}) collective-permute-start(bf16[33,32,128]{2,1,0:T(8,128)(2,1)S(1)} %get-tuple-element.172), channel_id=1, source_target_pairs={{0,1},{1,2},{2,3},{3,0},{4,5},{5,6},{6,7},{7,4},{8,9},{9,10},{10,1... | collective-permute-start | bytes 811016 | tf_op jit(solution)/shard_map/ppermute | solution.py:308
  414.4 19.1 %collective-permute-start.10 = (bf16[4,32,32,128]{3,2,1,0:T(8,128)(2,1)S(1)}, bf16[4,32,32,128]{3,2,1,0:T(8,128)(2,1)S(1)}, u32[]{:S(2)}, u32[]{:S(2)}) collective-permute-start(bf16[4,32,32,128]{3,2,1,0:T(8,128)(2,1)S(1)} %copy-done.2), channel_id=1, source_target_pairs={{0,4},{4,0},{8,12},{12,8},{16,20},{20,16},{24,28},{28,24},{32,36},... | collective-permute-start | bytes 3145736 | tf_op jit(solution)/shard_map/ppermute | solution.py:331
  (83 other events, 1273.4 us)
Sparse Core Ops, SparseCore 0:
  343.5 85.7 reduce-scatter.4
  443.1 78.6 reduce-scatter.2
